TPU v7x, 256 devices: a whole 4x4x8 slice. The times are simulated.
256 devices in a mesh: sweep: 8 (over y, core), layer: 32 (over z, x).
Axes of the slice: x: 4, y: 4, z: 8, core: 2. Of those that a mesh axis runs over, the one named last changes fastest.
Arguments:
- face_rhs: float32 [8, 16, 128, 384], P('sweep', None, 'layer'), may hold values from -6 to 6
- res_rows: float32 [131072, 384], P(('sweep', 'layer')), may hold values from -4 to 4
- row_owner: int32 [131072, 1], P(('sweep', 'layer')), may hold values from 0 to 31; in each aligned block of 512 rows (0 to 511, 512 to 1023, ...) at most 32 rows name the same one
- row_slot: int32 [131072], P(('sweep', 'layer')), may hold values from 0 to 63
- inv_blocks: bfloat16 [8, 128, 384, 384], P('sweep', 'layer'), may hold values from -0.3125 to 0.3125
- couple_in: bfloat16 [8, 1536, 49152], P('sweep', None, 'layer'), may hold values from -0.15625 to 0.15625
- couple_out: bfloat16 [8, 49152, 1536], P('sweep', 'layer'), may hold values from -0.02734375 to 0.02734375
Outputs:
- solved: float32 [8, 16, 128, 384], P('sweep', None, 'layer')
Inputs may be any that keep to these rules, and one draw needn't show every extreme that they name: `row_owner`: among the 512 rows of one device no owner is named by more than 32 rows, a bound that some block reaches.
All inputs are finite; a program needn't handle non-finite values.
Results may differ from a plain program's by a relative error of at most 0.02.
Values may be sent and summed in bfloat16 or wider, within the bound.
No kernel may reach another device: no remote copies, remote signals or barrier semaphores. Data moves between devices by JAX's collectives and lax.ppermute only.
A program may use at most 64 MiB of HBM per device.

v0:
```python
import jax
import jax.numpy as jnp
from jax import lax
from jax.sharding import PartitionSpec as P


def shifted(block, axis, distance):
    devices = range(lax.axis_size(axis))
    route = [(i - distance, i) for i in devices if i - distance in devices]
    return lax.ppermute(block, axis, route)


def on_device(face_rhs, res_rows, row_owner, row_slot, inv_blocks, couple_in, couple_out):
    group_size = lax.axis_size("layer")
    rhs_count = face_rhs.shape[1]
    face_dev = face_rhs.shape[2]
    face_width = face_rhs.shape[3]
    slot_count = rhs_count * face_dev
    row_total = res_rows.shape[0]
    owners = row_owner[:, 0]
    capacity = 2 * row_total // group_size
    matches = (owners[:, None] == jnp.arange(group_size, dtype=jnp.int32)[None, :]).astype(
        jnp.int32
    )
    earlier = jnp.cumsum(matches, axis=0) - matches
    position = jnp.sum(earlier * matches, axis=1)
    destination = owners * capacity + position
    send_rows = (
        jnp.zeros((group_size * capacity, face_width), jnp.float32).at[destination].set(res_rows)
    )
    send_slots = jnp.full((group_size * capacity,), -1, jnp.int32).at[destination].set(row_slot)
    got_rows, got_slots = (
        lax.all_to_all(
            send_rows.reshape(group_size, capacity, face_width),
            "layer",
            split_axis=0,
            concat_axis=0,
            tiled=True,
        ),
        lax.all_to_all(
            send_slots.reshape(group_size, capacity),
            "layer",
            split_axis=0,
            concat_axis=0,
            tiled=True,
        ),
    )
    one_hot = (jnp.arange(slot_count, dtype=jnp.int32)[:, None] == got_slots.reshape(1, -1)).astype(
        jnp.float32
    )
    added_rows = jnp.dot(one_hot, got_rows.reshape(-1, face_width), precision=lax.Precision.HIGHEST)
    assembled = face_rhs[0] + added_rows.reshape(rhs_count, face_dev, face_width)
    coupling_in = couple_in[0]
    coupling_out = couple_out[0]
    inverse = inv_blocks[0]
    sections = lax.axis_size("sweep")
    panel_in = jnp.zeros((rhs_count, coupling_in.shape[0]), jnp.bfloat16)
    solved = jnp.zeros_like(assembled)
    panel_part = jnp.zeros((rhs_count, coupling_in.shape[0]), jnp.float32)
    for step_index in range(sections):
        coupled = jnp.dot(panel_in, coupling_in, preferred_element_type=jnp.float32)
        local_part = (assembled - coupled.reshape(rhs_count, face_dev, face_width)).astype(
            jnp.bfloat16
        )
        solve_solved = jnp.einsum(
            "rfw,fwv->rfv", local_part, inverse, preferred_element_type=jnp.float32
        )
        flattened = solve_solved.astype(jnp.bfloat16).reshape(rhs_count, face_dev * face_width)
        solve_panel_part = jnp.dot(flattened, coupling_out, preferred_element_type=jnp.float32)
        solved = solve_solved
        panel_part = solve_panel_part
        if step_index + 1 < sections:
            summed = lax.psum(panel_part, "layer").astype(jnp.bfloat16)
            arrived = shifted(summed, "sweep", 1)
            panel_in = arrived
    return solved[None]


def solution(mesh):
    return jax.shard_map(
        on_device,
        mesh=mesh,
        in_specs=(
            P("sweep", None, "layer", None),
            P(("sweep", "layer"), None),
            P(("sweep", "layer"), None),
            P(("sweep", "layer")),
            P("sweep", "layer", None, None),
            P("sweep", None, "layer"),
            P("sweep", "layer", None),
        ),
        out_specs=P("sweep", None, "layer", None),
        check_vma=False,
    )
```

profile of v0, /device:TPU:1, one launch (start us, length us, event | category | flops | bytes accessed | tf_op | source)
XLA Modules:
  0.0 1123.9 jit_solution(9724480542182899194)
XLA Ops:
  7.0 11.9 %all-to-all-start = ((s32[32,1,32]{2,1,0:T(1,128)}), s32[32,1,32]{2,1,0:T(1,128)S(1)}, u32[]{:S(2)}, u32[]{:S(2)}) async-start(s32[32,1,32]{2,1,0:T(1,128)} %all_to_all.9), calls=%async_computation | async-start | bytes 32768 | tf_op jit(solution)/shard_map/all_to_all | solution.py:40
  18.9 4.0 scatter_custom_fusion.1
  22.9 4.5 all-to-all-done
  27.4 4.7 all-to-all-start.1
  33.4 35.1 %all-to-all-done.1 = f32[32,32,384]{2,1,0:T(8,128)S(1)} async-done(((f32[32,32,384]{2,1,0:T(8,128)}), f32[32,32,384]{2,1,0:T(8,128)S(1)}, u32[]{:S(2)}, u32[]{:S(2)}) %all-to-all-start.1) | async-done | bytes 1572896 | tf_op jit(solution)/shard_map/all_to_all | solution.py:33
  69.2 3.2 fusion.136
  75.5 112.3 %psum.49 = bf16[16,1536]{1,0:T(8,128)(2,1)S(1)} all-reduce(f32[16,1536]{1,0:T(8,128)S(1)} %fusion.28), channel_id=1, replica_groups=mesh['sweep'=8,'layer'=32] {'layer'}, use_global_device_ids=true, to_apply=%region_5.6 | all-reduce | flops 24576 | bytes 147456 | tf_op jit(solution)/shard_map/psum | solution.py:73
  187.8 34.2 %collective-permute-start = (bf16[16,1536]{1,0:T(8,128)(2,1)S(1)}, bf16[16,1536]{1,0:T(8,128)(2,1)S(1)}, u32[]{:S(2)}, u32[]{:S(2)}) collective-permute-start(bf16[16,1536]{1,0:T(8,128)(2,1)S(1)} %psum.49), channel_id=1, source_target_pairs={{0,32},{32,64},{64,96},{96,128},{128,160},{160,192},{192,224},{1,3... | collective-permute-start | bytes 147464 | tf_op jit(solution)/shard_map/ppermute | solution.py:10
  223.2 3.2 fusion.133
  229.5 110.7 %psum.50 = bf16[16,1536]{1,0:T(8,128)(2,1)S(1)} all-reduce(f32[16,1536]{1,0:T(8,128)S(1)} %fusion.26), channel_id=1, replica_groups=mesh['sweep'=8,'layer'=32] {'layer'}, use_global_device_ids=true, to_apply=%region_6.7 | all-reduce | flops 24576 | bytes 147456 | tf_op jit(solution)/shard_map/psum | solution.py:73
  340.2 31.3 %collective-permute-start.1 = (bf16[16,1536]{1,0:T(8,128)(2,1)S(1)}, bf16[16,1536]{1,0:T(8,128)(2,1)S(1)}, u32[]{:S(2)}, u32[]{:S(2)}) collective-permute-start(bf16[16,1536]{1,0:T(8,128)(2,1)S(1)} %psum.50), channel_id=1, source_target_pairs={{0,32},{32,64},{64,96},{96,128},{128,160},{160,192},{192,224},{1,3... | collective-permute-start | bytes 147464 | tf_op jit(solution)/shard_map/ppermute | solution.py:10
  372.6 3.2 fusion.130
  378.9 110.1 %psum.51 = bf16[16,1536]{1,0:T(8,128)(2,1)S(1)} all-reduce(f32[16,1536]{1,0:T(8,128)S(1)} %fusion.24), channel_id=1, replica_groups=mesh['sweep'=8,'layer'=32] {'layer'}, use_global_device_ids=true, to_apply=%region_7.8 | all-reduce | flops 24576 | bytes 147456 | tf_op jit(solution)/shard_map/psum | solution.py:73
  489.0 31.9 %collective-permute-start.2 = (bf16[16,1536]{1,0:T(8,128)(2,1)S(1)}, bf16[16,1536]{1,0:T(8,128)(2,1)S(1)}, u32[]{:S(2)}, u32[]{:S(2)}) collective-permute-start(bf16[16,1536]{1,0:T(8,128)(2,1)S(1)} %psum.51), channel_id=1, source_target_pairs={{0,32},{32,64},{64,96},{96,128},{128,160},{160,192},{192,224},{1,3... | collective-permute-start | bytes 147464 | tf_op jit(solution)/shard_map/ppermute | solution.py:10
  528.4 110.1 %psum.52 = bf16[16,1536]{1,0:T(8,128)(2,1)S(1)} all-reduce(f32[16,1536]{1,0:T(8,128)S(1)} %fusion.22), channel_id=1, replica_groups=mesh['sweep'=8,'layer'=32] {'layer'}, use_global_device_ids=true, to_apply=%region_8.9 | all-reduce | flops 24576 | bytes 147456 | tf_op jit(solution)/shard_map/psum | solution.py:73
  638.6 32.0 %collective-permute-start.3 = (bf16[16,1536]{1,0:T(8,128)(2,1)S(1)}, bf16[16,1536]{1,0:T(8,128)(2,1)S(1)}, u32[]{:S(2)}, u32[]{:S(2)}) collective-permute-start(bf16[16,1536]{1,0:T(8,128)(2,1)S(1)} %psum.52), channel_id=1, source_target_pairs={{0,32},{32,64},{64,96},{96,128},{128,160},{160,192},{192,224},{1,3... | collective-permute-start | bytes 147464 | tf_op jit(solution)/shard_map/ppermute | solution.py:10
  671.6 3.2 fusion.124
  677.9 110.4 %psum.53 = bf16[16,1536]{1,0:T(8,128)(2,1)S(1)} all-reduce(f32[16,1536]{1,0:T(8,128)S(1)} %fusion.20), channel_id=1, replica_groups=mesh['sweep'=8,'layer'=32] {'layer'}, use_global_device_ids=true, to_apply=%region_9.10 | all-reduce | flops 24576 | bytes 147456 | tf_op jit(solution)/shard_map/psum | solution.py:73
  788.2 31.6 %collective-permute-start.4 = (bf16[16,1536]{1,0:T(8,128)(2,1)S(1)}, bf16[16,1536]{1,0:T(8,128)(2,1)S(1)}, u32[]{:S(2)}, u32[]{:S(2)}) collective-permute-start(bf16[16,1536]{1,0:T(8,128)(2,1)S(1)} %psum.53), channel_id=1, source_target_pairs={{0,32},{32,64},{64,96},{96,128},{128,160},{160,192},{192,224},{1,3... | collective-permute-start | bytes 147464 | tf_op jit(solution)/shard_map/ppermute | solution.py:10
  827.3 110.5 %psum.54 = bf16[16,1536]{1,0:T(8,128)(2,1)S(1)} all-reduce(f32[16,1536]{1,0:T(8,128)S(1)} %fusion.18), channel_id=1, replica_groups=mesh['sweep'=8,'layer'=32] {'layer'}, use_global_device_ids=true, to_apply=%region_10.11 | all-reduce | flops 24576 | bytes 147456 | tf_op jit(solution)/shard_map/psum | solution.py:73
  937.8 31.5 %collective-permute-start.5 = (bf16[16,1536]{1,0:T(8,128)(2,1)S(1)}, bf16[16,1536]{1,0:T(8,128)(2,1)S(1)}, u32[]{:S(2)}, u32[]{:S(2)}) collective-permute-start(bf16[16,1536]{1,0:T(8,128)(2,1)S(1)} %psum.54), channel_id=1, source_target_pairs={{0,32},{32,64},{64,96},{96,128},{128,160},{160,192},{192,224},{1,3... | collective-permute-start | bytes 147464 | tf_op jit(solution)/shard_map/ppermute | solution.py:10
  976.8 110.7 %psum.55 = bf16[16,1536]{1,0:T(8,128)(2,1)S(1)} all-reduce(f32[16,1536]{1,0:T(8,128)S(1)} %fusion.16), channel_id=1, replica_groups=mesh['sweep'=8,'layer'=32] {'layer'}, use_global_device_ids=true, to_apply=%region_11.12 | all-reduce | flops 24576 | bytes 147456 | tf_op jit(solution)/shard_map/psum | solution.py:73
  1087.4 31.3 %collective-permute-start.6 = (bf16[16,1536]{1,0:T(8,128)(2,1)S(1)}, bf16[16,1536]{1,0:T(8,128)(2,1)S(1)}, u32[]{:S(2)}, u32[]{:S(2)}) collective-permute-start(bf16[16,1536]{1,0:T(8,128)(2,1)S(1)} %psum.55), channel_id=1, source_target_pairs={{0,32},{32,64},{64,96},{96,128},{128,160},{160,192},{192,224},{1,3... | collective-permute-start | bytes 147464 | tf_op jit(solution)/shard_map/ppermute | solution.py:10
  1120.0 3.2 fusion.46
  (43 shorter events, 48.7 us)
Async XLA Ops:
  0.0 69.2 %copy-start = (bf16[1,4,384,384]{3,2,1,0:T(8,128)(2,1)S(1)}, bf16[1,4,384,384]{3,2,1,0:T(8,128)(2,1)}, u32[]{:S(2)}) copy-start(bf16[1,4,384,384]{3,2,1,0:T(8,128)(2,1)} %param.11) | copy-start | bytes 3538948
  0.0 68.5 %copy-start.1 = (f32[1,16,4,384]{3,2,1,0:T(4,128)S(1)}, f32[1,16,4,384]{3,2,1,0:T(4,128)}, u32[]{:S(2)}) copy-start(f32[1,16,4,384]{3,2,1,0:T(4,128)} %param.7) | copy-start | bytes 294916
  7.0 20.4 %all-to-all-start = ((s32[32,1,32]{2,1,0:T(1,128)}), s32[32,1,32]{2,1,0:T(1,128)S(1)}, u32[]{:S(2)}, u32[]{:S(2)}) async-start(s32[32,1,32]{2,1,0:T(1,128)} %all_to_all.9), calls=%async_computation | async-start | bytes 32768 | tf_op jit(solution)/shard_map/all_to_all | solution.py:40
  27.4 41.1 %all-to-all-start.1 = ((f32[32,32,384]{2,1,0:T(8,128)}), f32[32,32,384]{2,1,0:T(8,128)S(1)}, u32[]{:S(2)}, u32[]{:S(2)}) async-start(f32[32,32,384]{2,1,0:T(8,128)} %bitcast.6), calls=%async_computation.1 | async-start | bytes 3145728 | tf_op jit(solution)/shard_map/all_to_all | solution.py:33
  187.8 35.4 %collective-permute-start = (bf16[16,1536]{1,0:T(8,128)(2,1)S(1)}, bf16[16,1536]{1,0:T(8,128)(2,1)S(1)}, u32[]{:S(2)}, u32[]{:S(2)}) collective-permute-start(bf16[16,1536]{1,0:T(8,128)(2,1)S(1)} %psum.49), channel_id=1, source_target_pairs={{0,32},{32,64},{64,96},{96,128},{128,160},{160,192},{192,224},{1,3... | collective-permute-start | bytes 147464 | tf_op jit(solution)/shard_map/ppermute | solution.py:10
  340.2 32.4 %collective-permute-start.1 = (bf16[16,1536]{1,0:T(8,128)(2,1)S(1)}, bf16[16,1536]{1,0:T(8,128)(2,1)S(1)}, u32[]{:S(2)}, u32[]{:S(2)}) collective-permute-start(bf16[16,1536]{1,0:T(8,128)(2,1)S(1)} %psum.50), channel_id=1, source_target_pairs={{0,32},{32,64},{64,96},{96,128},{128,160},{160,192},{192,224},{1,3... | collective-permute-start | bytes 147464 | tf_op jit(solution)/shard_map/ppermute | solution.py:10
  489.0 33.1 %collective-permute-start.2 = (bf16[16,1536]{1,0:T(8,128)(2,1)S(1)}, bf16[16,1536]{1,0:T(8,128)(2,1)S(1)}, u32[]{:S(2)}, u32[]{:S(2)}) collective-permute-start(bf16[16,1536]{1,0:T(8,128)(2,1)S(1)} %psum.51), channel_id=1, source_target_pairs={{0,32},{32,64},{64,96},{96,128},{128,160},{160,192},{192,224},{1,3... | collective-permute-start | bytes 147464 | tf_op jit(solution)/shard_map/ppermute | solution.py:10
  638.6 33.0 %collective-permute-start.3 = (bf16[16,1536]{1,0:T(8,128)(2,1)S(1)}, bf16[16,1536]{1,0:T(8,128)(2,1)S(1)}, u32[]{:S(2)}, u32[]{:S(2)}) collective-permute-start(bf16[16,1536]{1,0:T(8,128)(2,1)S(1)} %psum.52), channel_id=1, source_target_pairs={{0,32},{32,64},{64,96},{96,128},{128,160},{160,192},{192,224},{1,3... | collective-permute-start | bytes 147464 | tf_op jit(solution)/shard_map/ppermute | solution.py:10
  788.2 32.8 %collective-permute-start.4 = (bf16[16,1536]{1,0:T(8,128)(2,1)S(1)}, bf16[16,1536]{1,0:T(8,128)(2,1)S(1)}, u32[]{:S(2)}, u32[]{:S(2)}) collective-permute-start(bf16[16,1536]{1,0:T(8,128)(2,1)S(1)} %psum.53), channel_id=1, source_target_pairs={{0,32},{32,64},{64,96},{96,128},{128,160},{160,192},{192,224},{1,3... | collective-permute-start | bytes 147464 | tf_op jit(solution)/shard_map/ppermute | solution.py:10
  937.8 32.7 %collective-permute-start.5 = (bf16[16,1536]{1,0:T(8,128)(2,1)S(1)}, bf16[16,1536]{1,0:T(8,128)(2,1)S(1)}, u32[]{:S(2)}, u32[]{:S(2)}) collective-permute-start(bf16[16,1536]{1,0:T(8,128)(2,1)S(1)} %psum.54), channel_id=1, source_target_pairs={{0,32},{32,64},{64,96},{96,128},{128,160},{160,192},{192,224},{1,3... | collective-permute-start | bytes 147464 | tf_op jit(solution)/shard_map/ppermute | solution.py:10
  1087.4 32.5 %collective-permute-start.6 = (bf16[16,1536]{1,0:T(8,128)(2,1)S(1)}, bf16[16,1536]{1,0:T(8,128)(2,1)S(1)}, u32[]{:S(2)}, u32[]{:S(2)}) collective-permute-start(bf16[16,1536]{1,0:T(8,128)(2,1)S(1)} %psum.55), channel_id=1, source_target_pairs={{0,32},{32,64},{64,96},{96,128},{128,160},{160,192},{192,224},{1,3... | collective-permute-start | bytes 147464 | tf_op jit(solution)/shard_map/ppermute | solution.py:10
where the time goes:
time: 1130 us; the launch traced here: 1120 us
  blocking collectives  775 us (69%)
  starting transfers between devices  241 us (21%)
  matrix products  47.8 us (4%)
  waiting for transfers between devices  47.5 us (4%)
    psum x7, blocking collectives, on_device(): summed = lax.psum(panel_part, 'layer').astype(jnp.bfloat16)  775 us
    ppermute x7, starting transfers between devices, shifted(): return lax.ppermute(block, axis, route)  224 us
    all_to_all x1, waiting for transfers between devices, on_device(): lax.all_to_all(send_rows.reshape(group_size, capacity, face_width), 'laye...  35.1 us
    dot_general x8, matrix products, on_device(): jnp.einsum('rfw,fwv->rfv', local_part, inverse, preferred_element_type=jn...  25.7 us
  transfers between devices with their start and end apart: 9, of which 9 were waited for; matrix products, arithmetic and copies ran while one was open for 0% of the time, Pallas kernels for 0%

commit v1 on v0

--- a/solution.py
+++ b/solution.py
@@ -70,7 +70,7 @@
         solved = solve_solved
         panel_part = solve_panel_part
         if step_index + 1 < sections:
-            summed = lax.psum(panel_part, "layer").astype(jnp.bfloat16)
+            summed = jnp.sum(lax.all_gather(panel_part, "layer"), axis=0).astype(jnp.bfloat16)
             arrived = shifted(summed, "sweep", 1)
             panel_in = arrived
     return solved[None]

time: 1130 us -> 729 us (0.65)
  blocking collectives: 775 us -> 0 us
  waiting for transfers between devices: 47.5 us -> 564 us
  starting transfers between devices: 241 us -> 70.2 us
  other arithmetic: 4.15 us -> 18.5 us
  between operations: 0.18 us -> 13.7 us
    psum x7 -> x0, blocking collectives: 775 us -> none  [on_device(): summed = lax.psum(panel_part, 'layer').astype(jnp.bfloat16)]
    all_gather x0 -> x7, waiting for transfers between devices: none -> 516 us  [on_device(): lax.all_gather(panel_part, 'layer')]
    ppermute x7, starting transfers between devices: 224 us -> 53.3 us  [shifted(): return lax.ppermute(block, axis, route)]
    reduce_sum x0 -> x7, other arithmetic: none -> 14.3 us  [on_device(): jnp.sum(lax.all_gather(panel_part, 'layer'), axis=0).astype(jnp.bfloat16)]
  transfers between devices with their start and end apart: 9 -> 16, of which waited for: 9 -> 16; matrix products, arithmetic and copies ran while one was open for 0% -> 1% of each run, Pallas kernels for 0% -> 0%
where the time goes in v1:
time: 729 us; the launch traced here: 727 us
  waiting for transfers between devices  564 us (77%)
  starting transfers between devices  70.2 us (10%)
  matrix products  52.4 us (7%)
  other arithmetic  18.5 us (3%)
  between operations  13.7 us (2%)
  local copies, waits for them, and re-layouts  8.93 us (1%)
    all_gather x7, waiting for transfers between devices, on_device(): lax.all_gather(panel_part, 'layer')  516 us
    ppermute x7, starting transfers between devices, shifted(): return lax.ppermute(block, axis, route)  53.3 us
    all_to_all x1, waiting for transfers between devices, on_device(): lax.all_to_all(send_rows.reshape(group_size, capacity, face_width), 'laye...  35 us
    dot_general x7, matrix products, on_device(): jnp.dot(flattened, coupling_out, preferred_element_type=jnp.float32)  25.9 us
    dot_general x8, matrix products, on_device(): jnp.einsum('rfw,fwv->rfv', local_part, inverse, preferred_element_type=jn...  25.7 us
  transfers between devices with their start and end apart: 16, of which 16 were waited for; matrix products, arithmetic and copies ran while one was open for 1% of the time, Pallas kernels for 0%

profile of v1, /device:TPU:1, one launch (start us, length us, event | category | flops | bytes accessed | tf_op | source)
XLA Modules:
  0.0 727.5 jit_solution(15097511888904321015)
XLA Ops:
  13.5 11.9 %all-to-all-start = ((s32[32,1,32]{2,1,0:T(1,128)}), s32[32,1,32]{2,1,0:T(1,128)S(1)}, u32[]{:S(2)}, u32[]{:S(2)}) async-start(s32[32,1,32]{2,1,0:T(1,128)} %all_to_all.9), calls=%async_computation | async-start | bytes 32768 | tf_op jit(solution)/shard_map/all_to_all | solution.py:40
  25.4 4.0 scatter_custom_fusion.1
  29.4 4.5 all-to-all-done
  33.9 4.7 all-to-all-start.1
  40.0 35.0 %all-to-all-done.1 = f32[32,32,384]{2,1,0:T(8,128)S(1)} async-done(((f32[32,32,384]{2,1,0:T(8,128)}), f32[32,32,384]{2,1,0:T(8,128)S(1)}, u32[]{:S(2)}, u32[]{:S(2)}) %all-to-all-start.1) | async-done | bytes 1572896 | tf_op jit(solution)/shard_map/all_to_all | solution.py:33
  79.0 3.7 fusion.28
  82.7 76.5 %all-gather.15.cloned.1.call-done = f32[512,1536]{1,0:T(8,128)} async-done(((f32[16,1536]{1,0:T(8,128)}), f32[512,1536]{1,0:T(8,128)}) %all-gather.15.cloned.1.call-update) | async-done | bytes 3145744 | tf_op jit(solution)/shard_map/all_gather | solution.py:73
  161.3 7.6 %collective-permute-start = (bf16[16,1536]{1,0:T(8,128)(2,1)S(1)}, bf16[16,1536]{1,0:T(8,128)(2,1)S(1)}, u32[]{:S(2)}, u32[]{:S(2)}) collective-permute-start(bf16[16,1536]{1,0:T(8,128)(2,1)S(1)} %reduce_sum.76), channel_id=1, source_target_pairs={{0,32},{32,64},{64,96},{96,128},{128,160},{160,192},{192,224},{1,3... | collective-permute-start | bytes 147464 | tf_op jit(solution)/shard_map/ppermute | solution.py:10
  173.3 3.7 fusion.26
  177.0 73.3 %all-gather.17.cloned.1.call-done = f32[512,1536]{1,0:T(8,128)} async-done(((f32[16,1536]{1,0:T(8,128)}), f32[512,1536]{1,0:T(8,128)}) %all-gather.17.cloned.1.call-update) | async-done | bytes 3145744 | tf_op jit(solution)/shard_map/all_gather | solution.py:73
  252.4 7.6 %collective-permute-start.1 = (bf16[16,1536]{1,0:T(8,128)(2,1)S(1)}, bf16[16,1536]{1,0:T(8,128)(2,1)S(1)}, u32[]{:S(2)}, u32[]{:S(2)}) collective-permute-start(bf16[16,1536]{1,0:T(8,128)(2,1)S(1)} %reduce_sum.77), channel_id=1, source_target_pairs={{0,32},{32,64},{64,96},{96,128},{128,160},{160,192},{192,224},{1,3... | collective-permute-start | bytes 147464 | tf_op jit(solution)/shard_map/ppermute | solution.py:10
  268.1 73.3 %all-gather.19.cloned.1.call-done = f32[512,1536]{1,0:T(8,128)} async-done(((f32[16,1536]{1,0:T(8,128)}), f32[512,1536]{1,0:T(8,128)}) %all-gather.19.cloned.1.call-update) | async-done | bytes 3145744 | tf_op jit(solution)/shard_map/all_gather | solution.py:73
  343.5 7.6 %collective-permute-start.2 = (bf16[16,1536]{1,0:T(8,128)(2,1)S(1)}, bf16[16,1536]{1,0:T(8,128)(2,1)S(1)}, u32[]{:S(2)}, u32[]{:S(2)}) collective-permute-start(bf16[16,1536]{1,0:T(8,128)(2,1)S(1)} %reduce_sum.78), channel_id=1, source_target_pairs={{0,32},{32,64},{64,96},{96,128},{128,160},{160,192},{192,224},{1,3... | collective-permute-start | bytes 147464 | tf_op jit(solution)/shard_map/ppermute | solution.py:10
  355.5 3.7 fusion.22
  359.3 73.3 %all-gather.21.cloned.1.call-done = f32[512,1536]{1,0:T(8,128)} async-done(((f32[16,1536]{1,0:T(8,128)}), f32[512,1536]{1,0:T(8,128)}) %all-gather.21.cloned.1.call-update) | async-done | bytes 3145744 | tf_op jit(solution)/shard_map/all_gather | solution.py:73
  434.6 7.8 %collective-permute-start.3 = (bf16[16,1536]{1,0:T(8,128)(2,1)S(1)}, bf16[16,1536]{1,0:T(8,128)(2,1)S(1)}, u32[]{:S(2)}, u32[]{:S(2)}) collective-permute-start(bf16[16,1536]{1,0:T(8,128)(2,1)S(1)} %reduce_sum.79), channel_id=1, source_target_pairs={{0,32},{32,64},{64,96},{96,128},{128,160},{160,192},{192,224},{1,3... | collective-permute-start | bytes 147464 | tf_op jit(solution)/shard_map/ppermute | solution.py:10
  446.6 3.7 fusion.20
  450.4 73.3 %all-gather.23.cloned.1.call-done = f32[512,1536]{1,0:T(8,128)} async-done(((f32[16,1536]{1,0:T(8,128)}), f32[512,1536]{1,0:T(8,128)}) %all-gather.23.cloned.1.call-update) | async-done | bytes 3145744 | tf_op jit(solution)/shard_map/all_gather | solution.py:73
  525.7 7.6 %collective-permute-start.4 = (bf16[16,1536]{1,0:T(8,128)(2,1)S(1)}, bf16[16,1536]{1,0:T(8,128)(2,1)S(1)}, u32[]{:S(2)}, u32[]{:S(2)}) collective-permute-start(bf16[16,1536]{1,0:T(8,128)(2,1)S(1)} %reduce_sum.80), channel_id=1, source_target_pairs={{0,32},{32,64},{64,96},{96,128},{128,160},{160,192},{192,224},{1,3... | collective-permute-start | bytes 147464 | tf_op jit(solution)/shard_map/ppermute | solution.py:10
  537.7 3.7 fusion.18
  541.5 73.3 %all-gather.25.cloned.1.call-done = f32[512,1536]{1,0:T(8,128)} async-done(((f32[16,1536]{1,0:T(8,128)}), f32[512,1536]{1,0:T(8,128)}) %all-gather.25.cloned.1.call-update) | async-done | bytes 3145744 | tf_op jit(solution)/shard_map/all_gather | solution.py:73
  616.9 7.6 %collective-permute-start.5 = (bf16[16,1536]{1,0:T(8,128)(2,1)S(1)}, bf16[16,1536]{1,0:T(8,128)(2,1)S(1)}, u32[]{:S(2)}, u32[]{:S(2)}) collective-permute-start(bf16[16,1536]{1,0:T(8,128)(2,1)S(1)} %reduce_sum.81), channel_id=1, source_target_pairs={{0,32},{32,64},{64,96},{96,128},{128,160},{160,192},{192,224},{1,3... | collective-permute-start | bytes 147464 | tf_op jit(solution)/shard_map/ppermute | solution.py:10
  632.6 73.4 %all-gather.27.cloned.1.call-done = f32[512,1536]{1,0:T(8,128)} async-done(((f32[16,1536]{1,0:T(8,128)}), f32[512,1536]{1,0:T(8,128)}) %all-gather.27.cloned.1.call-update) | async-done | bytes 3145744 | tf_op jit(solution)/shard_map/all_gather | solution.py:73
  708.0 7.6 %collective-permute-start.6 = (bf16[16,1536]{1,0:T(8,128)(2,1)S(1)}, bf16[16,1536]{1,0:T(8,128)(2,1)S(1)}, u32[]{:S(2)}, u32[]{:S(2)}) collective-permute-start(bf16[16,1536]{1,0:T(8,128)(2,1)S(1)} %reduce_sum.82), channel_id=1, source_target_pairs={{0,32},{32,64},{64,96},{96,128},{128,160},{160,192},{192,224},{1,3... | collective-permute-start | bytes 147464 | tf_op jit(solution)/shard_map/ppermute | solution.py:10
  (64 shorter events, 65.5 us)
Async XLA Ops:
  6.5 69.2 %copy-start = (bf16[1,4,384,384]{3,2,1,0:T(8,128)(2,1)S(1)}, bf16[1,4,384,384]{3,2,1,0:T(8,128)(2,1)}, u32[]{:S(2)}) copy-start(bf16[1,4,384,384]{3,2,1,0:T(8,128)(2,1)} %param.11) | copy-start | bytes 3538948
  6.5 68.5 %copy-start.1 = (f32[1,16,4,384]{3,2,1,0:T(4,128)S(1)}, f32[1,16,4,384]{3,2,1,0:T(4,128)}, u32[]{:S(2)}) copy-start(f32[1,16,4,384]{3,2,1,0:T(4,128)} %param.7) | copy-start | bytes 294916
  13.5 20.4 %all-to-all-start = ((s32[32,1,32]{2,1,0:T(1,128)}), s32[32,1,32]{2,1,0:T(1,128)S(1)}, u32[]{:S(2)}, u32[]{:S(2)}) async-start(s32[32,1,32]{2,1,0:T(1,128)} %all_to_all.9), calls=%async_computation | async-start | bytes 32768 | tf_op jit(solution)/shard_map/all_to_all | solution.py:40
  33.9 41.1 %all-to-all-start.1 = ((f32[32,32,384]{2,1,0:T(8,128)}), f32[32,32,384]{2,1,0:T(8,128)S(1)}, u32[]{:S(2)}, u32[]{:S(2)}) async-start(f32[32,32,384]{2,1,0:T(8,128)} %bitcast.6), calls=%async_computation.1 | async-start | bytes 3145728 | tf_op jit(solution)/shard_map/all_to_all | solution.py:33
  38.7 120.6 %all-gather.15.cloned.1.call-start = ((), (), s32[]{:S(2)}) async-start(), calls=%async_computation.2 | async-start | bytes 3244032 | tf_op jit(solution)/shard_map/all_gather | solution.py:73
  82.7 167.6 %all-gather.17.cloned.1.call-start = ((), (), s32[]{:S(2)}) async-start(), calls=%async_computation.3 | async-start | bytes 3244032 | tf_op jit(solution)/shard_map/all_gather | solution.py:73
  161.3 8.7 %collective-permute-start = (bf16[16,1536]{1,0:T(8,128)(2,1)S(1)}, bf16[16,1536]{1,0:T(8,128)(2,1)S(1)}, u32[]{:S(2)}, u32[]{:S(2)}) collective-permute-start(bf16[16,1536]{1,0:T(8,128)(2,1)S(1)} %reduce_sum.76), channel_id=1, source_target_pairs={{0,32},{32,64},{64,96},{96,128},{128,160},{160,192},{192,224},{1,3... | collective-permute-start | bytes 147464 | tf_op jit(solution)/shard_map/ppermute | solution.py:10
  177.0 164.5 %all-gather.19.cloned.1.call-start = ((), (), s32[]{:S(2)}) async-start(), calls=%async_computation.4 | async-start | bytes 3244032 | tf_op jit(solution)/shard_map/all_gather | solution.py:73
  252.4 8.7 %collective-permute-start.1 = (bf16[16,1536]{1,0:T(8,128)(2,1)S(1)}, bf16[16,1536]{1,0:T(8,128)(2,1)S(1)}, u32[]{:S(2)}, u32[]{:S(2)}) collective-permute-start(bf16[16,1536]{1,0:T(8,128)(2,1)S(1)} %reduce_sum.77), channel_id=1, source_target_pairs={{0,32},{32,64},{64,96},{96,128},{128,160},{160,192},{192,224},{1,3... | collective-permute-start | bytes 147464 | tf_op jit(solution)/shard_map/ppermute | solution.py:10
  268.1 164.5 %all-gather.21.cloned.1.call-start = ((), (), s32[]{:S(2)}) async-start(), calls=%async_computation.5 | async-start | bytes 3244032 | tf_op jit(solution)/shard_map/all_gather | solution.py:73
  343.5 8.7 %collective-permute-start.2 = (bf16[16,1536]{1,0:T(8,128)(2,1)S(1)}, bf16[16,1536]{1,0:T(8,128)(2,1)S(1)}, u32[]{:S(2)}, u32[]{:S(2)}) collective-permute-start(bf16[16,1536]{1,0:T(8,128)(2,1)S(1)} %reduce_sum.78), channel_id=1, source_target_pairs={{0,32},{32,64},{64,96},{96,128},{128,160},{160,192},{192,224},{1,3... | collective-permute-start | bytes 147464 | tf_op jit(solution)/shard_map/ppermute | solution.py:10
  359.2 164.5 %all-gather.23.cloned.1.call-start = ((), (), s32[]{:S(2)}) async-start(), calls=%async_computation.6 | async-start | bytes 3244032 | tf_op jit(solution)/shard_map/all_gather | solution.py:73
  434.6 8.7 %collective-permute-start.3 = (bf16[16,1536]{1,0:T(8,128)(2,1)S(1)}, bf16[16,1536]{1,0:T(8,128)(2,1)S(1)}, u32[]{:S(2)}, u32[]{:S(2)}) collective-permute-start(bf16[16,1536]{1,0:T(8,128)(2,1)S(1)} %reduce_sum.79), channel_id=1, source_target_pairs={{0,32},{32,64},{64,96},{96,128},{128,160},{160,192},{192,224},{1,3... | collective-permute-start | bytes 147464 | tf_op jit(solution)/shard_map/ppermute | solution.py:10
  450.3 164.5 %all-gather.25.cloned.1.call-start = ((), (), s32[]{:S(2)}) async-start(), calls=%async_computation.7 | async-start | bytes 3244032 | tf_op jit(solution)/shard_map/all_gather | solution.py:73
  525.7 8.7 %collective-permute-start.4 = (bf16[16,1536]{1,0:T(8,128)(2,1)S(1)}, bf16[16,1536]{1,0:T(8,128)(2,1)S(1)}, u32[]{:S(2)}, u32[]{:S(2)}) collective-permute-start(bf16[16,1536]{1,0:T(8,128)(2,1)S(1)} %reduce_sum.80), channel_id=1, source_target_pairs={{0,32},{32,64},{64,96},{96,128},{128,160},{160,192},{192,224},{1,3... | collective-permute-start | bytes 147464 | tf_op jit(solution)/shard_map/ppermute | solution.py:10
  541.5 164.5 %all-gather.27.cloned.1.call-start = ((), (), s32[]{:S(2)}) async-start(), calls=%async_computation.8 | async-start | bytes 3244032 | tf_op jit(solution)/shard_map/all_gather | solution.py:73
  616.9 8.7 %collective-permute-start.5 = (bf16[16,1536]{1,0:T(8,128)(2,1)S(1)}, bf16[16,1536]{1,0:T(8,128)(2,1)S(1)}, u32[]{:S(2)}, u32[]{:S(2)}) collective-permute-start(bf16[16,1536]{1,0:T(8,128)(2,1)S(1)} %reduce_sum.81), channel_id=1, source_target_pairs={{0,32},{32,64},{64,96},{96,128},{128,160},{160,192},{192,224},{1,3... | collective-permute-start | bytes 147464 | tf_op jit(solution)/shard_map/ppermute | solution.py:10
  708.0 8.7 %collective-permute-start.6 = (bf16[16,1536]{1,0:T(8,128)(2,1)S(1)}, bf16[16,1536]{1,0:T(8,128)(2,1)S(1)}, u32[]{:S(2)}, u32[]{:S(2)}) collective-permute-start(bf16[16,1536]{1,0:T(8,128)(2,1)S(1)} %reduce_sum.82), channel_id=1, source_target_pairs={{0,32},{32,64},{64,96},{96,128},{128,160},{160,192},{192,224},{1,3... | collective-permute-start | bytes 147464 | tf_op jit(solution)/shard_map/ppermute | solution.py:10
Sparse Core Ops, SparseCore 0:
  82.8 76.3 all-gather.14
  177.1 73.1 all-gather.16
  268.2 73.1 all-gather.18
  359.3 73.1 all-gather.20
  450.5 73.1 all-gather.22
  541.6 73.1 all-gather.24
  632.7 73.1 all-gather.26
